TPU v7x, 256 devices: a whole 4x4x8 slice. The times are simulated.
256 devices in a mesh: feat: 8 (over y, core), dom: 32 (over z, x).
Axes of the slice: x: 4, y: 4, z: 8, core: 2. Of those that a mesh axis runs over, the one named last changes fastest.
Arguments:
- features: bfloat16 [8, 4096, 4096], P(None, 'dom', 'feat'), may hold values from -6 to 6
- w_one: bfloat16 [4096, 1024], P('feat'), may hold values from -0.09375 to 0.09375
- w_two: bfloat16 [1024, 512], replicated, may hold values from -0.25 to 0.25
- neighbor: int32 [8, 4096, 10], P('feat', 'dom'), may hold values from 0 to 383
- degree: int32 [8, 4096], P('feat', 'dom'), may hold values from 1 to 10
- send_rows: int32 [8, 1024, 8], P('feat', 'dom'), may hold values from 0 to 127
- grad_out: bfloat16 [8, 4096, 512], P('feat', 'dom'), may hold values from -6 to 6
Outputs:
- out_two: bfloat16 [8, 4096, 512], P('feat', 'dom')
- grad_one: float32 [4096, 1024], P('feat')
- grad_two: float32 [1024, 512], replicated
All inputs are finite; a program needn't handle non-finite values.
Results may differ from a plain program's by a relative error of at most 0.015.
Values may be sent and summed in bfloat16 or wider, within the bound.
No kernel may reach another device: no remote copies, remote signals or barrier semaphores. Data moves between devices by JAX's collectives and lax.ppermute only.
A program may use at most 64 MiB of HBM per device.

v0:
```python
import math
import jax
import jax.numpy as jnp
from jax import lax
from jax.sharding import PartitionSpec as P


def trade(buffer):
    return lax.all_to_all(buffer, "dom", split_axis=0, concat_axis=0, tiled=True)


def on_device(features, w_one, w_two, neighbor, degree, send_rows, grad_out):
    groups, nodes, cols = features.shape
    width = w_two.shape[1]
    nbrs = neighbor[0]
    degs = degree[0]
    sends = send_rows[0]
    parts = lax.axis_size("dom")
    fan = nbrs.shape[1]
    slots = jnp.arange(fan, dtype=jnp.int32)
    weight = (slots[None, :] < degs[:, None]).astype(jnp.float32) / degs[:, None].astype(
        jnp.float32
    )
    flat = features.reshape(groups * nodes, cols)

    def spread(values):
        boxes = values[sends]
        recv = trade(boxes)
        table = jnp.concatenate([values, recv.reshape(-1, values.shape[1])], axis=0)
        gathered = table[nbrs]
        return jnp.sum(gathered.astype(jnp.float32) * weight[..., None], axis=1)

    def gather_back(grads):
        span = grads.shape[1]
        terms = (weight[..., None] * grads[:, None, :]).reshape(-1, span)
        table = jnp.zeros((nodes + sends.size, span), jnp.float32).at[nbrs.reshape(-1)].add(terms)
        local = table[:nodes]
        outgoing = table[nodes:].astype(jnp.bfloat16).reshape(parts, sends.shape[1], span)
        returned = trade(outgoing)
        home = (
            jnp.zeros((nodes, span), jnp.float32)
            .at[sends.reshape(-1)]
            .add(returned.reshape(-1, span).astype(jnp.float32))
        )
        return local + home

    rows = flat
    proj = lax.psum_scatter(
        jnp.dot(rows, w_one, preferred_element_type=jnp.float32),
        "feat",
        scatter_dimension=0,
        tiled=True,
    )
    p_self = proj[:, :width]
    p_near = proj[:, width:].astype(jnp.bfloat16)
    pre = p_self + spread(p_near)
    hidden = (pre * jax.nn.sigmoid(pre)).astype(jnp.bfloat16)
    agg = spread(hidden).astype(jnp.bfloat16)
    joined = jnp.concatenate([hidden, agg], axis=-1)
    out = jnp.dot(joined, w_two, preferred_element_type=jnp.float32).astype(jnp.bfloat16)
    grads = grad_out[0]
    two_sum = lax.dot_general(
        joined, grads, (((0,), (0,)), ((), ())), preferred_element_type=jnp.float32
    )
    dcat = lax.dot_general(
        grads, w_two, (((1,), (1,)), ((), ())), preferred_element_type=jnp.float32
    )
    d_hidden = dcat[:, :width] + gather_back(dcat[:, width:])
    sig = jax.nn.sigmoid(pre)
    d_pre = d_hidden * sig * (1.0 + pre * (1.0 - sig))
    d_near = gather_back(d_pre)
    d_proj = jnp.concatenate([d_pre, d_near], axis=-1).astype(jnp.bfloat16)
    rows = flat
    one_sum = lax.dot_general(
        rows,
        lax.all_gather(d_proj, "feat", axis=0, tiled=True),
        (((0,), (0,)), ((), ())),
        preferred_element_type=jnp.float32,
    )
    one_sum = lax.psum(one_sum.astype(jnp.bfloat16), "dom").astype(jnp.float32)
    two_sum = lax.psum(two_sum, ("feat", "dom"))
    scale = 1.0 / math.sqrt(groups * nodes * parts)
    return (out[None], one_sum * scale, two_sum * scale)


def solution(mesh):
    in_specs = (
        P(None, "dom", "feat"),
        P("feat", None),
        P(),
        P("feat", "dom", None),
        P("feat", "dom"),
        P("feat", "dom", None),
        P("feat", "dom", None),
    )
    out_specs = (P("feat", "dom", None), P("feat", None), P())
    return jax.shard_map(
        on_device, mesh=mesh, in_specs=in_specs, out_specs=out_specs, check_vma=False
    )
```

profile of v0, /device:TPU:8, one launch (start us, length us, event | category | flops | bytes accessed | tf_op | source)
XLA Modules:
  0.0 582.7 jit_solution(4482622993260259353)
XLA Ops:
  7.2 1.2 copy-done
  8.4 4.4 fusion.26
  12.8 0.7 copy-done.6
  13.5 0.1 copy.13
  13.6 0.1 reshape_squeeze.8
  13.7 0.3 copy-done.1
  14.0 0.5 fusion.20
  14.5 2.5 mul.73
  17.0 4.5 mul.74
  21.6 0.1 convert_divide_fusion
  21.7 0.1 div.23
  21.9 13.1 %scatter_custom_fusion = f32[384,512]{1,0:T(8,128)S(1)} fusion(s32[1280]{0:T(1024)S(1)} %fusion.22, f32[1280,512]{1,0:T(8,128)} %mul.74, f32[1280]{0:T(1024)S(1)} %div.23, f32[]{:T(128)} %constant.9.clone.1), kind=kCustom, calls=%fused_computation.12 | custom fusion | flops 1310720 | bytes 3416068 | tf_op jit(solution)/shard_map/scatter-add | solution.py:36
  34.9 0.7 fusion.14
  35.7 11.3 %all-to-all-start.2 = ((bf16[32,8,512]{2,1,0:T(8,128)(2,1)}), bf16[32,8,512]{2,1,0:T(8,128)(2,1)S(1)}, u32[]{:S(2)}, u32[]{:S(2)}) async-start(bf16[32,8,512]{2,1,0:T(8,128)(2,1)} %fusion.14), calls=%async_computation.3 | async-start | bytes 524288 | tf_op jit(solution)/shard_map/all_to_all | solution.py:9
  47.2 0.1 copy.12
  47.3 0.1 reshape.219
  47.5 5.2 reduce-scatter.2.cloned.1.call-done
  52.7 1.0 slice.65
  53.7 1.9 gather_fusion
  55.5 4.2 all-to-all-done.2
  59.7 5.7 all-to-all-start
  65.6 2.4 scatter_custom_fusion.1
  68.0 10.6 %all-to-all-done = bf16[32,8,512]{2,1,0:T(8,128)(2,1)S(1)} async-done(((bf16[32,8,512]{2,1,0:T(8,128)(2,1)}), bf16[32,8,512]{2,1,0:T(8,128)(2,1)S(1)}, u32[]{:S(2)}, u32[]{:S(2)}) %all-to-all-start) | async-done | bytes 262176 | tf_op jit(solution)/shard_map/all_to_all | solution.py:9
  78.7 4.1 gather_fusion.1
  82.8 2.1 reshape.277
  84.9 3.2 multiply_reduce_fusion.1
  88.1 0.1 fusion.25
  88.3 2.5 mul.79
  90.8 4.5 mul.80
  95.3 13.1 %scatter_custom_fusion.2 = f32[384,512]{1,0:T(8,128)S(1)} fusion(s32[1280]{0:T(1024)S(1)} %fusion.22, f32[1280,512]{1,0:T(8,128)} %mul.80, f32[1280]{0:T(1024)S(1)} %div.23, f32[]{:T(128)} %constant.9.clone.1), kind=kCustom, calls=%fused_computation.10 | custom fusion | flops 1310720 | bytes 3416068 | tf_op jit(solution)/shard_map/scatter-add | solution.py:36
  108.3 0.7 fusion.15
  109.1 3.9 all-to-all-start.3
  113.0 12.2 %all-to-all-done.3 = bf16[32,8,512]{2,1,0:T(8,128)(2,1)S(1)} async-done(((bf16[32,8,512]{2,1,0:T(8,128)(2,1)}), bf16[32,8,512]{2,1,0:T(8,128)(2,1)S(1)}, u32[]{:S(2)}, u32[]{:S(2)}) %all-to-all-start.3) | async-done | bytes 262176 | tf_op jit(solution)/shard_map/all_to_all | solution.py:9
  125.3 2.2 scatter_custom_fusion.3
  127.6 0.7 pad_maximum_fusion.3
  128.4 1.2 gather_fusion.2
  129.5 15.7 %all_to_all.20 = bf16[32,8,512]{2,1,0:T(8,128)(2,1)S(1)} all-to-all(bf16[32,8,512]{2,1,0:T(8,128)(2,1)S(1)} %bitcast.50), channel_id=1, replica_groups=mesh['feat'=8,'dom'=32] {'dom'}, dimensions={0} | all-to-all | bytes 524288 | tf_op jit(solution)/shard_map/all_to_all | solution.py:9
  145.3 4.1 gather_fusion.3
  149.4 2.1 reshape.278
  151.6 3.2 multiply_reduce_fusion
  154.8 1.8 fusion.18
  156.7 3.9 fusion.4
  160.7 1.0 fusion.7
  161.6 259.2 %all-reduce.5.cloned.1.call-done = f32[1024,512]{1,0:T(8,128)} async-done(((f32[1024,512]{1,0:T(8,128)}), f32[1024,512]{1,0:T(8,128)}) %all-reduce.5.cloned.1.call-update) | async-done | bytes 2097168 | tf_op jit(solution)/shard_map/psum | solution.py:81
  420.8 3.2 broadcast_multiply_fusion
  423.9 148.9 %all-reduce.3.cloned.1.call-done = bf16[512,1024]{0,1:T(8,128)(2,1)} async-done(((bf16[512,1024]{0,1:T(8,128)(2,1)}), bf16[512,1024]{0,1:T(8,128)(2,1)}) %all-reduce.3.cloned.1.call-update) | async-done | bytes 1048592 | tf_op jit(solution)/shard_map/psum | solution.py:80
  572.8 1.5 convert_multiply_fusion
  574.4 1.8 copy.15
  (41 shorter events, 0.8 us)
Async XLA Ops:
  7.2 1.2 copy-start
  7.2 45.5 %reduce-scatter.2.cloned.1.call-start = ((), (), s32[]{:S(2)}) async-start(), calls=%async_computation.5 | async-start | bytes 4718592 | tf_op jit(solution)/shard_map/reduce_scatter | solution.py:48
  12.8 0.7 copy-start.6
  12.8 1.2 copy-start.1
  12.8 1.2 copy-start.3
  17.0 4.5 copy-start.8
  21.6 25.4 %copy-start.7 = (s32[1,32,8]{1,2,0:T(8,128)S(1)}, s32[1,32,8]{1,2,0:T(8,128)}, u32[]{:S(2)}) copy-start(s32[1,32,8]{1,2,0:T(8,128)} %param.12) | copy-start | bytes 3076
  35.7 24.0 %all-to-all-start.2 = ((bf16[32,8,512]{2,1,0:T(8,128)(2,1)}), bf16[32,8,512]{2,1,0:T(8,128)(2,1)S(1)}, u32[]{:S(2)}, u32[]{:S(2)}) async-start(bf16[32,8,512]{2,1,0:T(8,128)(2,1)} %fusion.14), calls=%async_computation.3 | async-start | bytes 524288 | tf_op jit(solution)/shard_map/all_to_all | solution.py:9
  59.7 18.9 %all-to-all-start = ((bf16[32,8,512]{2,1,0:T(8,128)(2,1)}), bf16[32,8,512]{2,1,0:T(8,128)(2,1)S(1)}, u32[]{:S(2)}, u32[]{:S(2)}) async-start(bf16[32,8,512]{2,1,0:T(8,128)(2,1)} %bitcast.2), calls=%async_computation.1 | async-start | bytes 524288 | tf_op jit(solution)/shard_map/all_to_all | solution.py:9
  84.9 3.3 copy-start.5
  109.1 16.2 %all-to-all-start.3 = ((bf16[32,8,512]{2,1,0:T(8,128)(2,1)}), bf16[32,8,512]{2,1,0:T(8,128)(2,1)S(1)}, u32[]{:S(2)}, u32[]{:S(2)}) async-start(bf16[32,8,512]{2,1,0:T(8,128)(2,1)} %fusion.15), calls=%async_computation.4 | async-start | bytes 524288 | tf_op jit(solution)/shard_map/all_to_all | solution.py:9
  113.0 43.7 %all-gather.2.cloned.1.call-start = ((), (), s32[]{:S(2)}) async-start(), calls=%async_computation.6 | async-start | bytes 2359296 | tf_op jit(solution)/shard_map/all_gather | solution.py:76
  128.3 292.5 %all-reduce.5.cloned.1.call-start = ((), (), s32[]{:S(2)}) async-start(), calls=%async_computation.8 | async-start | bytes 4194304 | tf_op jit(solution)/shard_map/psum | solution.py:81
  151.6 3.2 copy-start.4
  156.6 4.0 copy-start.2
  156.6 416.2 %all-reduce.3.cloned.1.call-start = ((), (), s32[]{:S(2)}) async-start(), calls=%async_computation.7 | async-start | bytes 2097152 | tf_op jit(solution)/shard_map/psum | solution.py:80
Sparse Core Ops, SparseCore 0:
  12.9 39.6 reduce-scatter.1
  128.4 23.6 all-gather.1
  158.1 262.6 all-reduce.4
  424.7 148.1 all-reduce.2
where the time goes:
time: 583 us
  waiting for transfers between devices  440 us (75%)
  other arithmetic  43.1 us (7%)
  local copies, waits for them, and re-layouts  36.9 us (6%)
  starting transfers between devices  21 us (4%)
  blocking collectives  15.7 us (3%)
  between operations  14.1 us (2%)
  matrix products  11.5 us (2%)
    psum x1, waiting for transfers between devices, on_device(): two_sum = lax.psum(two_sum, ('feat', 'dom'))  259 us
    psum x1, waiting for transfers between devices, on_device(): one_sum = lax.psum(one_sum.astype(jnp.bfloat16), 'dom').astype(jnp.float32)  149 us
    all_to_all x3, waiting for transfers between devices, trade(): lax.all_to_all(buffer, 'dom', split_axis=0, concat_axis=0, tiled=True)  27 us
    scatter-add x2, other arithmetic, gather_back(): jnp.zeros((nodes + sends.size, span), jnp.float32).at[nbrs.reshape(-1)]  26.1 us
    all_to_all x3, starting transfers between devices, trade(): lax.all_to_all(buffer, 'dom', split_axis=0, concat_axis=0, tiled=True)  20.8 us
    all_to_all x1, blocking collectives, trade(): lax.all_to_all(buffer, 'dom', split_axis=0, concat_axis=0, tiled=True)  15.7 us
    mul x4, local copies, waits for them, and re-layouts, gather_back(): terms = (weight[..., None] * grads[:, None, :]).reshape(-1, span)  14 us
  transfers between devices with their start and end apart: 7, of which 6 were waited for; matrix products, arithmetic and copies ran while one was open for 8% of the time, Pallas kernels for 0%

commit v1 on v0

--- a/solution.py
+++ b/solution.py
@@ -78,7 +78,7 @@
         preferred_element_type=jnp.float32,
     )
     one_sum = lax.psum(one_sum.astype(jnp.bfloat16), "dom").astype(jnp.float32)
-    two_sum = lax.psum(two_sum, ("feat", "dom"))
+    two_sum = lax.psum(lax.psum(two_sum, "dom"), "feat")
     scale = 1.0 / math.sqrt(groups * nodes * parts)
     return (out[None], one_sum * scale, two_sum * scale)
 

time: 583 us -> 537 us (0.921)
  waiting for transfers between devices: 440 us -> 393 us
    psum x1 -> x2, waiting for transfers between devices: 259 us -> 179 us  [on_device(): two_sum = lax.psum(lax.psum(two_sum, 'dom'), 'feat')]
    all_gather x1, waiting for transfers between devices: 0.02 us -> 26.2 us  [on_device(): lax.all_gather(d_proj, 'feat', axis=0, tiled=True)]
  transfers between devices with their start and end apart: 7 -> 8, of which waited for: 6 -> 8; matrix products, arithmetic and copies ran while one was open for 8% -> 11% of each run, Pallas kernels for 0% -> 0%
where the time goes in v1:
time: 537 us
  waiting for transfers between devices  393 us (73%)
  other arithmetic  43.9 us (8%)
  local copies, waits for them, and re-layouts  36.8 us (7%)
  starting transfers between devices  21 us (4%)
  blocking collectives  16 us (3%)
  between operations  14.1 us (3%)
  matrix products  11.5 us (2%)
    psum x2, waiting for transfers between devices, on_device(): two_sum = lax.psum(lax.psum(two_sum, 'dom'), 'feat')  179 us
    psum x1, waiting for transfers between devices, on_device(): one_sum = lax.psum(one_sum.astype(jnp.bfloat16), 'dom').astype(jnp.float32)  152 us
    all_to_all x3, waiting for transfers between devices, trade(): lax.all_to_all(buffer, 'dom', split_axis=0, concat_axis=0, tiled=True)  30 us
    scatter-add x2, other arithmetic, gather_back(): jnp.zeros((nodes + sends.size, span), jnp.float32).at[nbrs.reshape(-1)]  26.3 us
    all_gather x1, waiting for transfers between devices, on_device(): lax.all_gather(d_proj, 'feat', axis=0, tiled=True)  26.2 us
    all_to_all x3, starting transfers between devices, trade(): lax.all_to_all(buffer, 'dom', split_axis=0, concat_axis=0, tiled=True)  20.8 us
    all_to_all x1, blocking collectives, trade(): lax.all_to_all(buffer, 'dom', split_axis=0, concat_axis=0, tiled=True)  16 us
    mul x4, local copies, waits for them, and re-layouts, gather_back(): terms = (weight[..., None] * grads[:, None, :]).reshape(-1, span)  14 us
  transfers between devices with their start and end apart: 8, of which 8 were waited for; matrix products, arithmetic and copies ran while one was open for 11% of the time, Pallas kernels for 0%

profile of v1, /device:TPU:8, one launch (start us, length us, event | category | flops | bytes accessed | tf_op | source)
XLA Modules:
  0.0 536.5 jit_solution(1468334069499661558)
XLA Ops:
  7.2 1.2 copy-done
  8.4 4.4 fusion.26
  12.8 0.7 copy-done.7
  13.6 0.1 reshape_squeeze.8
  13.7 0.3 copy-done.1
  14.0 0.5 fusion.20
  14.5 2.5 mul.73
  17.0 4.5 mul.74
  21.7 0.1 div.23
  21.9 13.1 %scatter_custom_fusion = f32[384,512]{1,0:T(8,128)S(1)} fusion(s32[1280]{0:T(1024)S(1)} %fusion.22, f32[1280,512]{1,0:T(8,128)} %mul.74, f32[1280]{0:T(1024)S(1)} %div.23, f32[]{:T(128)} %constant.9.clone.1), kind=kCustom, calls=%fused_computation.12 | custom fusion | flops 1310720 | bytes 3416068 | tf_op jit(solution)/shard_map/scatter-add | solution.py:36
  34.9 0.7 fusion.14
  35.7 11.3 %all-to-all-start.2 = ((bf16[32,8,512]{2,1,0:T(8,128)(2,1)}), bf16[32,8,512]{2,1,0:T(8,128)(2,1)S(1)}, u32[]{:S(2)}, u32[]{:S(2)}) async-start(bf16[32,8,512]{2,1,0:T(8,128)(2,1)} %fusion.14), calls=%async_computation.3 | async-start | bytes 524288 | tf_op jit(solution)/shard_map/all_to_all | solution.py:9
  47.2 0.1 copy.12
  47.3 0.1 reshape.219
  47.5 5.2 reduce-scatter.2.cloned.1.call-done
  52.7 1.0 slice.65
  53.7 1.9 gather_fusion
  55.5 4.2 all-to-all-done.2
  59.7 5.7 %all-to-all-start = ((bf16[32,8,512]{2,1,0:T(8,128)(2,1)}), bf16[32,8,512]{2,1,0:T(8,128)(2,1)S(1)}, u32[]{:S(2)}, u32[]{:S(2)}) async-start(bf16[32,8,512]{2,1,0:T(8,128)(2,1)} %bitcast.2), calls=%async_computation.1 | async-start | bytes 524288 | tf_op jit(solution)/shard_map/all_to_all | solution.py:9
  65.6 2.4 scatter_custom_fusion.1
  68.1 10.5 %all-to-all-done = bf16[32,8,512]{2,1,0:T(8,128)(2,1)S(1)} async-done(((bf16[32,8,512]{2,1,0:T(8,128)(2,1)}), bf16[32,8,512]{2,1,0:T(8,128)(2,1)S(1)}, u32[]{:S(2)}, u32[]{:S(2)}) %all-to-all-start) | async-done | bytes 262176 | tf_op jit(solution)/shard_map/all_to_all | solution.py:9
  78.7 4.1 gather_fusion.1
  82.8 2.1 reshape.277
  84.9 3.2 multiply_reduce_fusion.1
  88.1 0.8 fusion.25
  88.9 1.2 gather_fusion.2
  90.1 16.0 %all_to_all.20 = bf16[32,8,512]{2,1,0:T(8,128)(2,1)S(1)} all-to-all(bf16[32,8,512]{2,1,0:T(8,128)(2,1)S(1)} %bitcast.50), channel_id=1, replica_groups=mesh['feat'=8,'dom'=32] {'dom'}, dimensions={0} | all-to-all | bytes 524288 | tf_op jit(solution)/shard_map/all_to_all | solution.py:9
  106.1 4.1 gather_fusion.3
  110.2 2.1 reshape.278
  112.3 3.2 multiply_reduce_fusion
  115.6 1.8 fusion.18
  117.4 2.5 mul.79
  119.8 4.5 mul.80
  124.4 13.2 %scatter_custom_fusion.2 = f32[384,512]{1,0:T(8,128)S(1)} fusion(s32[1280]{0:T(1024)S(1)} %fusion.22, f32[1280,512]{1,0:T(8,128)} %mul.80, f32[1280]{0:T(1024)S(1)} %div.23, f32[]{:T(128)} %constant.9.clone.1), kind=kCustom, calls=%fused_computation.10 | custom fusion | flops 1310720 | bytes 3416068 | tf_op jit(solution)/shard_map/scatter-add | solution.py:36
  137.6 0.7 fusion.15
  138.3 3.9 all-to-all-start.3
  142.3 15.3 %all-to-all-done.3 = bf16[32,8,512]{2,1,0:T(8,128)(2,1)S(1)} async-done(((bf16[32,8,512]{2,1,0:T(8,128)(2,1)}), bf16[32,8,512]{2,1,0:T(8,128)(2,1)S(1)}, u32[]{:S(2)}, u32[]{:S(2)}) %all-to-all-start.3) | async-done | bytes 262176 | tf_op jit(solution)/shard_map/all_to_all | solution.py:9
  157.6 2.2 scatter_custom_fusion.3
  159.9 0.7 pad_maximum_fusion.3
  160.7 112.1 %all-reduce.6.cloned.1.call-done = f32[1024,512]{1,0:T(8,128)} async-done(((f32[1024,512]{1,0:T(8,128)}), f32[1024,512]{1,0:T(8,128)}) %all-reduce.6.cloned.1.call-update) | async-done | bytes 2097168 | tf_op jit(solution)/shard_map/psum | solution.py:81
  272.9 26.2 %all-gather.2.cloned.1.call-done = bf16[1024,1024]{1,0:T(8,128)(2,1)} async-done(((bf16[128,1024]{1,0:T(8,128)(2,1)}), bf16[1024,1024]{1,0:T(8,128)(2,1)}) %all-gather.2.cloned.1.call-update) | async-done | bytes 2097168 | tf_op jit(solution)/shard_map/all_gather | solution.py:76
  299.0 3.8 fusion.4
  302.9 1.0 fusion.7
  303.9 67.1 %all-reduce.8.cloned.1.call-done = f32[1024,512]{1,0:T(8,128)} async-done(((f32[1024,512]{1,0:T(8,128)}), f32[1024,512]{1,0:T(8,128)}) %all-reduce.8.cloned.1.call-update) | async-done | bytes 2097168 | tf_op jit(solution)/shard_map/psum | solution.py:81
  371.0 3.2 broadcast_multiply_fusion
  374.2 152.5 %all-reduce.4.cloned.1.call-done = bf16[512,1024]{0,1:T(8,128)(2,1)} async-done(((bf16[512,1024]{0,1:T(8,128)(2,1)}), bf16[512,1024]{0,1:T(8,128)(2,1)}) %all-reduce.4.cloned.1.call-update) | async-done | bytes 1048592 | tf_op jit(solution)/shard_map/psum | solution.py:80
  526.7 1.5 convert_multiply_fusion
  528.2 1.8 copy.15
  (46 shorter events, 1.1 us)
Async XLA Ops:
  7.2 1.2 copy-start
  7.2 45.5 %reduce-scatter.2.cloned.1.call-start = ((), (), s32[]{:S(2)}) async-start(), calls=%async_computation.5 | async-start | bytes 4718592 | tf_op jit(solution)/shard_map/reduce_scatter | solution.py:48
  12.8 0.7 copy-start.7
  12.8 1.2 copy-start.1
  12.8 1.2 copy-start.4
  17.0 4.5 copy-start.9
  21.6 25.4 %copy-start.8 = (s32[1,32,8]{1,2,0:T(8,128)S(1)}, s32[1,32,8]{1,2,0:T(8,128)}, u32[]{:S(2)}) copy-start(s32[1,32,8]{1,2,0:T(8,128)} %param.12) | copy-start | bytes 3076
  35.7 24.0 %all-to-all-start.2 = ((bf16[32,8,512]{2,1,0:T(8,128)(2,1)}), bf16[32,8,512]{2,1,0:T(8,128)(2,1)S(1)}, u32[]{:S(2)}, u32[]{:S(2)}) async-start(bf16[32,8,512]{2,1,0:T(8,128)(2,1)} %fusion.14), calls=%async_computation.3 | async-start | bytes 524288 | tf_op jit(solution)/shard_map/all_to_all | solution.py:9
  59.7 18.9 %all-to-all-start = ((bf16[32,8,512]{2,1,0:T(8,128)(2,1)}), bf16[32,8,512]{2,1,0:T(8,128)(2,1)S(1)}, u32[]{:S(2)}, u32[]{:S(2)}) async-start(bf16[32,8,512]{2,1,0:T(8,128)(2,1)} %bitcast.2), calls=%async_computation.1 | async-start | bytes 524288 | tf_op jit(solution)/shard_map/all_to_all | solution.py:9
  65.4 207.4 %all-reduce.6.cloned.1.call-start = ((), (), s32[]{:S(2)}) async-start(), calls=%async_computation.8 | async-start | bytes 4194304 | tf_op jit(solution)/shard_map/psum | solution.py:81
  84.9 3.3 copy-start.6
  112.3 3.2 copy-start.5
  124.3 35.5 %copy-start.3 = (bf16[128,512]{1,0:T(8,128)(2,1)S(1)}, bf16[128,512]{1,0:T(8,128)(2,1)}, u32[]{:S(2)}) copy-start(bf16[128,512]{1,0:T(8,128)(2,1)} %get-tuple-element.9) | copy-start | bytes 393220
  138.3 19.3 %all-to-all-start.3 = ((bf16[32,8,512]{2,1,0:T(8,128)(2,1)}), bf16[32,8,512]{2,1,0:T(8,128)(2,1)S(1)}, u32[]{:S(2)}, u32[]{:S(2)}) async-start(bf16[32,8,512]{2,1,0:T(8,128)(2,1)} %fusion.15), calls=%async_computation.4 | async-start | bytes 524288 | tf_op jit(solution)/shard_map/all_to_all | solution.py:9
  142.2 156.8 %all-gather.2.cloned.1.call-start = ((), (), s32[]{:S(2)}) async-start(), calls=%async_computation.6 | async-start | bytes 2359296 | tf_op jit(solution)/shard_map/all_gather | solution.py:76
  160.6 210.4 %all-reduce.8.cloned.1.call-start = ((), (), s32[]{:S(2)}) async-start(), calls=%async_computation.9 | async-start | bytes 4194304 | tf_op jit(solution)/shard_map/psum | solution.py:81
  272.8 30.1 %copy-start.2 = (bf16[1024,512]{1,0:T(8,128)(2,1)S(1)}, bf16[1024,512]{1,0:T(8,128)(2,1)}, u32[]{:S(2)}) copy-start(bf16[1024,512]{1,0:T(8,128)(2,1)} %param.9) | copy-start | bytes 3145732
  272.8 253.8 %all-reduce.4.cloned.1.call-start = ((), (), s32[]{:S(2)}) async-start(), calls=%async_computation.7 | async-start | bytes 2097152 | tf_op jit(solution)/shard_map/psum | solution.py:80
Sparse Core Ops, SparseCore 0:
  12.9 39.6 reduce-scatter.1
  117.5 155.2 all-reduce.5
  275.4 23.6 all-gather.1
  301.4 69.5 all-reduce.7
  375.3 151.3 all-reduce.3
